TPU v7x, 512 devices: a whole 4x8x8 slice. The times are simulated.
512 devices in a mesh: expert: 32 (over y_lo, z, core), dp: 16 (over y_hi, x).
Axes of the slice: x: 4, y: 8 (y_hi: 4, y_lo: 2; y = y_hi * 2 + y_lo), z: 8, core: 2. Of those that a mesh axis runs over, the one named last changes fastest.
Arguments:
- tokens: bfloat16 [65536, 3584], P(('expert', 'dp')), may hold values from -6 to 6
- expert_ids: int32 [65536, 8], P(('expert', 'dp')), may hold values from 0 to 255, all different within a row
- gate_probs: float32 [65536, 8], P(('expert', 'dp')), may hold values from 0.02 to 0.5
- out_grad: bfloat16 [65536, 3584], P(('expert', 'dp')), may hold values from -6 to 6
- w_gate: bfloat16 [32, 1024, 3584], P('expert', 'dp'), may hold values from -0.09375 to 0.09375
- w_up: bfloat16 [32, 1024, 3584], P('expert', 'dp'), may hold values from -0.09375 to 0.09375
- w_down: bfloat16 [32, 1024, 3584], P('expert', 'dp'), may hold values from -0.1875 to 0.1875
Outputs:
- grad_gate: bfloat16 [32, 1024, 3584], P('expert', 'dp')
- grad_up: bfloat16 [32, 1024, 3584], P('expert', 'dp')
- grad_down: bfloat16 [32, 1024, 3584], P('expert', 'dp')
All inputs are finite; a program needn't handle non-finite values.
Results may differ from a plain program's by a relative error of at most 0.0058.
Values may be sent and summed in bfloat16 or wider, within the bound.
A program may use at most 64 MiB of HBM per device.

v0:
```python
import jax
import jax.numpy as jnp
from jax import lax
from jax.sharding import PartitionSpec as P

CAP = 2


def local_factors(rows_x, rows_dy, weight_gate, weight_up, weight_down):
    contract = (((1,), (1,)), ((), ()))
    gate_pre = lax.dot_general(rows_x, weight_gate, contract, preferred_element_type=jnp.float32)
    up_pre = lax.dot_general(rows_x, weight_up, contract, preferred_element_type=jnp.float32)
    back_grad = lax.dot_general(rows_dy, weight_down, contract, preferred_element_type=jnp.float32)
    sig_gate = jax.nn.sigmoid(gate_pre)
    act_gate = gate_pre * sig_gate
    hidden = (act_gate * up_pre).astype(jnp.bfloat16)
    d_gate = (back_grad * up_pre * sig_gate * (1.0 + gate_pre * (1.0 - sig_gate))).astype(
        jnp.bfloat16
    )
    d_up = (back_grad * act_gate).astype(jnp.bfloat16)
    return (d_gate, d_up, hidden)


def outer_sum(factor, rows):
    return lax.dot_general(
        factor, rows, (((0,), (0,)), ((), ())), preferred_element_type=jnp.float32
    )


def local(tokens, expert_ids, gate_probs, out_grad, w_gate, w_up, w_down):
    n_expert = lax.axis_size("expert")
    experts_all = w_gate.shape[0] * n_expert
    tok_rows, top_count = expert_ids.shape
    feature_count = tokens.shape[1]
    flat_ids = expert_ids.reshape(-1)
    expert_range = jnp.arange(experts_all, dtype=jnp.int32)
    onehot = (flat_ids[:, None] == expert_range[None, :]).astype(jnp.int32)
    before = jnp.cumsum(onehot, axis=0) - onehot
    slot_rank = jnp.sum(before * onehot, axis=1)
    kept_mask = (flat_ids < experts_all) & (slot_rank < CAP)
    slot_index = jnp.where(kept_mask, flat_ids * CAP + slot_rank, -1)
    slot_range = jnp.arange(experts_all * CAP, dtype=jnp.int32)
    matches = (slot_index[None, :] == slot_range[:, None]).astype(jnp.float32)
    matches = matches.reshape(experts_all * CAP, tok_rows, top_count)
    picker = jnp.sum(matches, axis=2).astype(jnp.bfloat16)
    slot_prob = jnp.sum(matches * gate_probs[None, :, :], axis=(1, 2))
    sent_x = jnp.dot(picker, tokens, preferred_element_type=jnp.float32).astype(jnp.bfloat16)
    sent_dy = (
        jnp.dot(picker, out_grad, preferred_element_type=jnp.float32) * slot_prob[:, None]
    ).astype(jnp.bfloat16)
    sent_x = sent_x.reshape(experts_all, CAP, feature_count)
    sent_dy = sent_dy.reshape(experts_all, CAP, feature_count)
    recv_x, recv_dy = (
        lax.all_to_all(sent_x, "expert", split_axis=0, concat_axis=0, tiled=True),
        lax.all_to_all(sent_dy, "expert", split_axis=0, concat_axis=0, tiled=True),
    )
    rows_x = recv_x.reshape(-1, feature_count)
    rows_dy = recv_dy.reshape(-1, feature_count)
    piece_x = lax.all_gather(rows_x, "dp", axis=0, tiled=True)
    piece_dy = lax.all_gather(rows_dy, "dp", axis=0, tiled=True)
    d_gate, d_up, hidden = local_factors(piece_x, piece_dy, w_gate[0], w_up[0], w_down[0])
    term_gate = outer_sum(d_gate, piece_x)
    term_up = outer_sum(d_up, piece_x)
    term_down = outer_sum(hidden, piece_dy)
    return (
        term_gate.astype(jnp.bfloat16)[None],
        term_up.astype(jnp.bfloat16)[None],
        term_down.astype(jnp.bfloat16)[None],
    )


def solution(mesh):
    in_specs = (
        P(("expert", "dp"), None),
        P(("expert", "dp"), None),
        P(("expert", "dp"), None),
        P(("expert", "dp"), None),
        P("expert", "dp", None),
        P("expert", "dp", None),
        P("expert", "dp", None),
    )
    out_specs = (P("expert", "dp", None), P("expert", "dp", None), P("expert", "dp", None))
    return jax.shard_map(local, mesh=mesh, in_specs=in_specs, out_specs=out_specs, check_vma=False)
```

profile of v0, /device:TPU:1, one launch (start us, length us, event | category | flops | bytes accessed | tf_op | source)
XLA Modules:
  0.0 293.1 jit_solution(2632505541616493926)
XLA Ops:
  7.2 0.0 copy-start
  7.2 0.0 copy-start.3
  7.2 0.0 all-gather.5.cloned.1.call-start
  7.2 0.9 copy.30
  8.1 0.1 eq.43
  8.2 0.1 eq.39
  8.3 9.0 %reduce-window.6 = s32[32,8,128]{2,1,0:T(8,128)S(1)} reduce-window(s32[32,8,128]{2,1,0:T(8,128)S(1)} %fusion.15, s32[]{:T(128)} %constant.4.clone.1), window={size=1x1x128 pad=0_0x0_0x127_0}, to_apply=%region_0.0 | reduce-window | flops 4161536 | bytes 262148 | tf_op jit(solution)/shard_map/reduce-window
  17.3 0.1 slice.8
  17.4 0.1 copy.32
  17.6 0.1 copy.33
  17.7 0.1 broadcast_add_fusion
  17.8 0.1 reduce_sum.30
  18.0 0.7 add_select_fusion
  18.7 1.2 select_reduce_fusion
  19.9 0.0 copy-done
  19.9 0.3 convolution_convert_fusion.3
  20.2 0.2 reshape.64
  20.4 27.1 %all_to_all.10 = bf16[32,2,3584]{2,1,0:T(2,128)(2,1)S(1)} all-to-all(bf16[32,2,3584]{2,1,0:T(2,128)(2,1)S(1)} %reshape.64), channel_id=1, replica_groups=mesh['expert'=32,'dp'=16] {'expert'}, dimensions={0} | all-to-all | bytes 917504 | tf_op jit(solution)/shard_map/all_to_all | solution.py:54
  47.5 0.0 copy-start.4
  47.5 0.9 reshape.65
  48.4 0.0 all-gather.5.cloned.1.call-update
  48.4 0.0 all-gather.3.cloned.1.call-start
  48.5 1.5 fusion
  49.9 0.2 reshape.62
  50.1 19.5 %all_to_all.11 = bf16[32,2,3584]{2,1,0:T(2,128)(2,1)S(1)} all-to-all(bf16[32,2,3584]{2,1,0:T(2,128)(2,1)S(1)} %reshape.62), channel_id=1, replica_groups=mesh['expert'=32,'dp'=16] {'expert'}, dimensions={0} | all-to-all | bytes 917504 | tf_op jit(solution)/shard_map/all_to_all | solution.py:55
  69.6 0.9 reshape.63
  70.6 0.0 all-gather.3.cloned.1.call-update
  70.6 0.0 copy-start.5
  70.6 85.9 %all-gather.5.cloned.1.call-done = bf16[1024,3584]{1,0:T(8,128)(2,1)} async-done(((bf16[64,3584]{1,0:T(8,128)(2,1)}), bf16[1024,3584]{1,0:T(8,128)(2,1)}) %all-gather.5.cloned.1.call-update) | async-done | bytes 7340048 | tf_op jit(solution)/shard_map/all_gather | solution.py:59
  156.5 0.0 copy-done.3
  156.5 0.0 copy-start.1
  156.5 5.5 %fusion.4 = f32[1024,64]{0,1:T(8,128)S(1)} fusion(bf16[1024,3584]{1,0:T(8,128)(2,1)} %all-gather.5.cloned.1.call-done, bf16[1,64,3584]{2,1,0:T(8,128)(2,1)S(1)} %copy-done.3), kind=kOutput, calls=%fused_computation.9 | convolution fusion | flops 469762048 | bytes 8060928 | tf_op jit(solution)/shard_map/dot_general | solution.py:11
  162.1 0.0 copy-done.4
  162.1 0.0 copy-done.1
  162.1 2.3 fusion.6
  164.4 106.6 %all-gather.3.cloned.1.call-done = bf16[1024,3584]{1,0:T(8,128)(2,1)} async-done(((bf16[64,3584]{1,0:T(8,128)(2,1)}), bf16[1024,3584]{1,0:T(8,128)(2,1)}) %all-gather.3.cloned.1.call-update) | async-done | bytes 7340048 | tf_op jit(solution)/shard_map/all_gather | solution.py:60
  271.0 0.0 copy-done.5
  271.0 0.0 copy-start.2
  271.0 5.5 %fusion.8 = f32[1024,64]{0,1:T(8,128)S(1)} fusion(bf16[1024,3584]{1,0:T(8,128)(2,1)} %all-gather.3.cloned.1.call-done, bf16[1,64,3584]{2,1,0:T(8,128)(2,1)S(1)} %copy-done.5), kind=kOutput, calls=%fused_computation.13 | convolution fusion | flops 469762048 | bytes 8060928 | tf_op jit(solution)/shard_map/dot_general | solution.py:13
  276.6 0.0 copy-done.2
  276.6 0.0 slice-start
  276.6 2.1 fusion.3
  278.7 0.0 slice-start.1
  278.7 5.4 %fusion.1 = bf16[1,64,3584]{2,1,0:T(8,128)(2,1)} fusion(bf16[1024,3584]{1,0:T(8,128)(2,1)} %all-gather.5.cloned.1.call-done, f32[1024,64]{0,1:T(8,128)S(1)} %fusion.4, f32[1024,64]{0,1:T(8,128)S(1)} %fusion.8, f32[1024,64]{0,1:T(8,128)S(1)} %fusion.6), kind=kOutput, calls=%fused_computation.6 | convolution fusion | flops 470646784 | bytes 8585216 | tf_op jit(solution)/shard_map/dot_general | solution.py:25
  284.1 0.0 slice-done
  284.1 0.0 slice-done.1
  284.1 2.1 fusion.2
  (6 shorter events, 0.1 us)
Async XLA Ops:
  7.2 12.8 %copy-start = (bf16[128,3584]{1,0:T(8,128)(2,1)S(1)}, bf16[128,3584]{1,0:T(8,128)(2,1)}, u32[]{:S(2)}) copy-start(bf16[128,3584]{1,0:T(8,128)(2,1)} %param.7) | copy-start | bytes 2752516
  7.2 149.3 %copy-start.3 = (bf16[1,64,3584]{2,1,0:T(8,128)(2,1)S(1)}, bf16[1,64,3584]{2,1,0:T(8,128)(2,1)}, u32[]{:S(2)}) copy-start(bf16[1,64,3584]{2,1,0:T(8,128)(2,1)} %param.11) | copy-start | bytes 1376260
  7.2 149.3 %all-gather.5.cloned.1.call-start = ((), (), s32[]{:S(2)}) async-start(), calls=%async_computation.3 | async-start | bytes 7798784 | tf_op jit(solution)/shard_map/all_gather | solution.py:59
  47.5 114.6 %copy-start.4 = (bf16[1,64,3584]{2,1,0:T(8,128)(2,1)S(1)}, bf16[1,64,3584]{2,1,0:T(8,128)(2,1)}, u32[]{:S(2)}) copy-start(bf16[1,64,3584]{2,1,0:T(8,128)(2,1)} %param.12) | copy-start | bytes 1376260
  48.4 222.6 %all-gather.3.cloned.1.call-start = ((), (), s32[]{:S(2)}) async-start(), calls=%async_computation.2 | async-start | bytes 7798784 | tf_op jit(solution)/shard_map/all_gather | solution.py:60
  70.6 200.4 %copy-start.5 = (bf16[1,64,3584]{2,1,0:T(8,128)(2,1)S(1)}, bf16[1,64,3584]{2,1,0:T(8,128)(2,1)}, u32[]{:S(2)}) copy-start(bf16[1,64,3584]{2,1,0:T(8,128)(2,1)} %param.13) | copy-start | bytes 1376260
  156.5 5.6 %copy-start.1 = (bf16[1024,3584]{1,0:T(8,128)(2,1)S(1)}, bf16[1024,3584]{1,0:T(8,128)(2,1)}, u32[]{:S(2)}) copy-start(bf16[1024,3584]{1,0:T(8,128)(2,1)} %all-gather.5.cloned.1.call-done) | copy-start | bytes 22020100
  271.0 5.5 %copy-start.2 = (bf16[1024,3584]{1,0:T(8,128)(2,1)S(1)}, bf16[1024,3584]{1,0:T(8,128)(2,1)}, u32[]{:S(2)}) copy-start(bf16[1024,3584]{1,0:T(8,128)(2,1)} %all-gather.3.cloned.1.call-done) | copy-start | bytes 22020100
  276.6 7.5 %slice-start = ((s8[7340032]{0:T(1024)(128)(4,1)}), s8[4194304]{0:T(1024)(128)(4,1)S(1)}, s32[]{:S(2)}) async-start(s8[7340032]{0:T(1024)(128)(4,1)} %bitcast.43), calls=%async_computation.4 | async-start | bytes 8388608
  278.7 5.4 %slice-start.1 = ((s8[7340032]{0:T(1024)(128)(4,1)}), s8[3145728]{0:T(1024)(128)(4,1)S(1)}, s32[]{:S(2)}) async-start(s8[7340032]{0:T(1024)(128)(4,1)} %bitcast.43), calls=%async_computation.5 | async-start | bytes 6291456
Sparse Core Ops, SparseCore 0:
  48.6 107.9 all-gather.4
  160.1 110.8 all-gather.2
where the time goes:
time: 293 us
  waiting for transfers between devices  193 us (66%)
  blocking collectives  46.6 us (16%)
  matrix products  24.7 us (8%)
  between operations  14.2 us (5%)
  other arithmetic  11.2 us (4%)
  local copies, waits for them, and re-layouts  3.76 us (1%)
    all_gather x1, waiting for transfers between devices, local(): piece_dy = lax.all_gather(rows_dy, 'dp', axis=0, tiled=True)  107 us
    all_gather x1, waiting for transfers between devices, local(): piece_x = lax.all_gather(rows_x, 'dp', axis=0, tiled=True)  85.9 us
    all_to_all x1, blocking collectives, local(): lax.all_to_all(sent_x, 'expert', split_axis=0, concat_axis=0, tiled=True)  27.1 us
    all_to_all x1, blocking collectives, local(): lax.all_to_all(sent_dy, 'expert', split_axis=0, concat_axis=0, tiled=True)  19.5 us
    dot_general x3, matrix products, outer_sum(): lax.dot_general(factor, rows, (((0,), (0,)), ((), ())), preferred_element...  9.65 us
    another operation x3, other arithmetic  9.15 us
  transfers between devices with their start and end apart: 2, of which 2 were waited for; matrix products, arithmetic and copies ran while one was open for 4% of the time, Pallas kernels for 0%

commit v1 on v0

--- a/solution.py
+++ b/solution.py
@@ -57,7 +57,9 @@
     rows_x = recv_x.reshape(-1, feature_count)
     rows_dy = recv_dy.reshape(-1, feature_count)
     piece_x = lax.all_gather(rows_x, "dp", axis=0, tiled=True)
-    piece_dy = lax.all_gather(rows_dy, "dp", axis=0, tiled=True)
+    piece_dy = jnp.concatenate(
+        lax.all_to_all(jnp.stack([rows_dy] * lax.axis_size("dp")), "dp", 0, 0), axis=0
+    )
     d_gate, d_up, hidden = local_factors(piece_x, piece_dy, w_gate[0], w_up[0], w_down[0])
     term_gate = outer_sum(d_gate, piece_x)
     term_up = outer_sum(d_up, piece_x)

time: 293 us -> 352 us (1.20)
  the two profiles are of different devices: /device:TPU:1 before, /device:TPU:493 now
where the time goes in v1:
time: 352 us
  waiting for transfers between devices  271 us (77%)
  matrix products  24.5 us (7%)
  starting transfers between devices  22.4 us (6%)
  between operations  14.2 us (4%)
  other arithmetic  11.2 us (3%)
  local copies, waits for them, and re-layouts  8.22 us (2%)
    all_to_all x1, waiting for transfers between devices, local(): lax.all_to_all(jnp.stack([rows_dy] * lax.axis_size('dp')), 'dp', 0, 0)  249 us
    all_to_all x1, waiting for transfers between devices, local(): lax.all_to_all(sent_x, 'expert', split_axis=0, concat_axis=0, tiled=True)  12.3 us
    all_to_all x1, waiting for transfers between devices, local(): lax.all_to_all(sent_dy, 'expert', split_axis=0, concat_axis=0, tiled=True)  10.1 us
    dot_general x3, matrix products, outer_sum(): lax.dot_general(factor, rows, (((0,), (0,)), ((), ())), preferred_element...  9.49 us
    all_to_all x1, starting transfers between devices, local(): lax.all_to_all(jnp.stack([rows_dy] * lax.axis_size('dp')), 'dp', 0, 0)  9.2 us
    another operation x3, other arithmetic  9.15 us
    all_to_all x1, starting transfers between devices, local(): lax.all_to_all(sent_x, 'expert', split_axis=0, concat_axis=0, tiled=True)  7.26 us
  transfers between devices with their start and end apart: 4, of which 3 were waited for; matrix products, arithmetic and copies ran while one was open for 3% of the time, Pallas kernels for 0%

profile of v1, /device:TPU:493, one launch (start us, length us, event | category | flops | bytes accessed | tf_op | source)
XLA Modules:
  0.0 351.9 jit_solution(14152359529279201841)
XLA Ops:
  7.2 0.0 copy-start
  7.2 0.9 copy.30
  8.0 0.1 eq.43
  8.1 0.1 eq.39
  8.3 9.0 %reduce-window.6 = s32[32,8,128]{2,1,0:T(8,128)S(1)} reduce-window(s32[32,8,128]{2,1,0:T(8,128)S(1)} %fusion.15, s32[]{:T(128)} %constant.4.clone.1), window={size=1x1x128 pad=0_0x0_0x127_0}, to_apply=%region_0.0 | reduce-window | flops 4161536 | bytes 262148 | tf_op jit(solution)/shard_map/reduce-window
  17.3 0.1 slice.8
  17.4 0.1 copy.32
  17.5 0.1 copy.33
  17.6 0.1 broadcast_add_fusion
  17.8 0.1 reduce_sum.30
  17.9 0.7 add_select_fusion
  18.6 1.2 select_reduce_fusion
  19.9 0.0 copy-done
  19.9 0.3 fusion
  20.1 0.9 reshape.64
  21.1 5.9 %all-to-all-start = ((bf16[32,2,3584]{2,1,0:T(2,128)(2,1)}), bf16[32,2,3584]{2,1,0:T(2,128)(2,1)S(1)}, u32[]{:S(2)}, u32[]{:S(2)}) async-start(bf16[32,2,3584]{2,1,0:T(2,128)(2,1)} %reshape.64), calls=%async_computation | async-start | bytes 917504 | tf_op jit(solution)/shard_map/all_to_all | solution.py:55
  27.0 1.4 convolution_convert_fusion.3
  28.5 0.9 reshape.66
  29.4 10.1 %all-to-all-done = bf16[32,2,3584]{2,1,0:T(2,128)(2,1)S(1)} async-done(((bf16[32,2,3584]{2,1,0:T(2,128)(2,1)}), bf16[32,2,3584]{2,1,0:T(2,128)(2,1)S(1)}, u32[]{:S(2)}, u32[]{:S(2)}) %all-to-all-start) | async-done | bytes 458784 | tf_op jit(solution)/shard_map/all_to_all | solution.py:55
  39.5 7.3 %all-to-all-start.2 = ((bf16[32,2,3584]{2,1,0:T(2,128)(2,1)}), bf16[32,2,3584]{2,1,0:T(2,128)(2,1)S(1)}, u32[]{:S(2)}, u32[]{:S(2)}) async-start(bf16[32,2,3584]{2,1,0:T(2,128)(2,1)} %reshape.66), calls=%async_computation.2 | async-start | bytes 917504 | tf_op jit(solution)/shard_map/all_to_all | solution.py:54
  46.8 0.2 stack_reshape.2
  46.9 12.3 %all-to-all-done.2 = bf16[32,2,3584]{2,1,0:T(2,128)(2,1)S(1)} async-done(((bf16[32,2,3584]{2,1,0:T(2,128)(2,1)}), bf16[32,2,3584]{2,1,0:T(2,128)(2,1)S(1)}, u32[]{:S(2)}, u32[]{:S(2)}) %all-to-all-start.2) | async-done | bytes 458784 | tf_op jit(solution)/shard_map/all_to_all | solution.py:54
  59.2 3.7 %stack.3 = bf16[16,64,3584]{2,1,0:T(8,128)(2,1)} broadcast(bf16[64,3584]{1,0:T(8,128)(2,1)S(1)} %stack_reshape.2), dimensions={1,2} | broadcast | bytes 7798784 | tf_op jit(solution)/shard_map/stack | solution.py:61
  63.0 0.0 copy-start.2
  63.0 9.2 %all-to-all-start.1 = ((bf16[16,64,3584]{2,1,0:T(8,128)(2,1)}), bf16[16,64,3584]{2,1,0:T(8,128)(2,1)}, u32[]{:S(2)}, u32[]{:S(2)}) async-start(bf16[16,64,3584]{2,1,0:T(8,128)(2,1)} %stack.3), calls=%async_computation.1 | async-start | bytes 14680064 | tf_op jit(solution)/shard_map/all_to_all | solution.py:61
  72.2 0.0 copy-start.3
  72.2 0.0 all-gather.2.cloned.1.call-start
  72.2 0.9 reshape.67
  73.2 0.0 all-gather.2.cloned.1.call-update
  73.2 249.0 %all-to-all-done.1 = bf16[16,64,3584]{2,1,0:T(8,128)(2,1)} async-done(((bf16[16,64,3584]{2,1,0:T(8,128)(2,1)}), bf16[16,64,3584]{2,1,0:T(8,128)(2,1)}, u32[]{:S(2)}, u32[]{:S(2)}) %all-to-all-start.1) | async-done | bytes 7340064 | tf_op jit(solution)/shard_map/all_to_all | solution.py:61
  322.2 0.0 copy-done.2
  322.2 0.0 copy-start.4
  322.2 5.4 %fusion.8 = f32[1024,64]{0,1:T(8,128)S(1)} fusion(bf16[1024,3584]{1,0:T(8,128)(2,1)} %bitcast.2, bf16[1,64,3584]{2,1,0:T(8,128)(2,1)S(1)} %copy-done.2), kind=kOutput, calls=%fused_computation.13 | convolution fusion | flops 469762048 | bytes 8060928 | tf_op jit(solution)/shard_map/dot_general | solution.py:13
  327.7 0.0 all-gather.2.cloned.1.call-done
  327.7 0.0 copy-done.3
  327.7 0.0 copy-start.1
  327.7 5.5 %fusion.4 = f32[1024,64]{0,1:T(8,128)S(1)} fusion(bf16[1024,3584]{1,0:T(8,128)(2,1)} %all-gather.2.cloned.1.call-done, bf16[1,64,3584]{2,1,0:T(8,128)(2,1)S(1)} %copy-done.3), kind=kOutput, calls=%fused_computation.9 | convolution fusion | flops 469762048 | bytes 8060928 | tf_op jit(solution)/shard_map/dot_general | solution.py:11
  333.3 0.0 copy-done.4
  333.3 0.0 copy-done.1
  333.3 2.3 fusion.6
  335.6 5.2 %fusion.3 = bf16[1,64,3584]{2,1,0:T(8,128)(2,1)} fusion(bf16[1024,3584]{1,0:T(8,128)(2,1)} %bitcast.2, f32[1024,64]{0,1:T(8,128)S(1)} %fusion.6, f32[1024,64]{0,1:T(8,128)S(1)} %fusion.4), kind=kOutput, calls=%fused_computation.8 | convolution fusion | flops 470384640 | bytes 8323072 | tf_op jit(solution)/shard_map/dot_general | solution.py:25
  340.8 2.2 fusion.1
  343.0 2.1 fusion.2
  (5 shorter events, 0.1 us)
Async XLA Ops:
  7.2 12.7 %copy-start = (bf16[128,3584]{1,0:T(8,128)(2,1)S(1)}, bf16[128,3584]{1,0:T(8,128)(2,1)}, u32[]{:S(2)}) copy-start(bf16[128,3584]{1,0:T(8,128)(2,1)} %param.10) | copy-start | bytes 2752516
  21.1 18.4 %all-to-all-start = ((bf16[32,2,3584]{2,1,0:T(2,128)(2,1)}), bf16[32,2,3584]{2,1,0:T(2,128)(2,1)S(1)}, u32[]{:S(2)}, u32[]{:S(2)}) async-start(bf16[32,2,3584]{2,1,0:T(2,128)(2,1)} %reshape.64), calls=%async_computation | async-start | bytes 917504 | tf_op jit(solution)/shard_map/all_to_all | solution.py:55
  39.5 19.7 %all-to-all-start.2 = ((bf16[32,2,3584]{2,1,0:T(2,128)(2,1)}), bf16[32,2,3584]{2,1,0:T(2,128)(2,1)S(1)}, u32[]{:S(2)}, u32[]{:S(2)}) async-start(bf16[32,2,3584]{2,1,0:T(2,128)(2,1)} %reshape.66), calls=%async_computation.2 | async-start | bytes 917504 | tf_op jit(solution)/shard_map/all_to_all | solution.py:54
  63.0 259.3 %copy-start.2 = (bf16[1,64,3584]{2,1,0:T(8,128)(2,1)S(1)}, bf16[1,64,3584]{2,1,0:T(8,128)(2,1)}, u32[]{:S(2)}) copy-start(bf16[1,64,3584]{2,1,0:T(8,128)(2,1)} %param.13) | copy-start | bytes 1376260
  63.0 259.3 %all-to-all-start.1 = ((bf16[16,64,3584]{2,1,0:T(8,128)(2,1)}), bf16[16,64,3584]{2,1,0:T(8,128)(2,1)}, u32[]{:S(2)}, u32[]{:S(2)}) async-start(bf16[16,64,3584]{2,1,0:T(8,128)(2,1)} %stack.3), calls=%async_computation.1 | async-start | bytes 14680064 | tf_op jit(solution)/shard_map/all_to_all | solution.py:61
  72.2 255.5 %copy-start.3 = (bf16[1,64,3584]{2,1,0:T(8,128)(2,1)S(1)}, bf16[1,64,3584]{2,1,0:T(8,128)(2,1)}, u32[]{:S(2)}) copy-start(bf16[1,64,3584]{2,1,0:T(8,128)(2,1)} %param.11) | copy-start | bytes 1376260
  72.2 255.5 %all-gather.2.cloned.1.call-start = ((), (), s32[]{:S(2)}) async-start(), calls=%async_computation.3 | async-start | bytes 7798784 | tf_op jit(solution)/shard_map/all_gather | solution.py:59
  322.2 11.0 %copy-start.4 = (bf16[1,64,3584]{2,1,0:T(8,128)(2,1)S(1)}, bf16[1,64,3584]{2,1,0:T(8,128)(2,1)}, u32[]{:S(2)}) copy-start(bf16[1,64,3584]{2,1,0:T(8,128)(2,1)} %param.12) | copy-start | bytes 1376260
  327.7 5.6 %copy-start.1 = (bf16[1024,3584]{1,0:T(8,128)(2,1)S(1)}, bf16[1024,3584]{1,0:T(8,128)(2,1)}, u32[]{:S(2)}) copy-start(bf16[1024,3584]{1,0:T(8,128)(2,1)} %all-gather.2.cloned.1.call-done) | copy-start | bytes 22020100
Sparse Core Ops, SparseCore 0:
  76.6 229.6 all-gather.1
